TPU v7x, 128 devices: a whole 4x4x4 slice. The times are simulated.
128 devices in a mesh: gx: 8 (over z, core), gy: 16 (over y, x).
Axes of the slice: x: 4, y: 4, z: 4, core: 2. Of those that a mesh axis runs over, the one named last changes fastest.
Arguments:
- tiles: bfloat16 [24576, 128, 128], P(('gx', 'gy')), may hold values from -6 to 6
- tile_rows: int32 [24576], P(('gx', 'gy')), may hold values from 0 to 63, as said below
- tile_cols: int32 [24576], P(('gx', 'gy')), may hold values from 0 to 255
- tile_counts: int32 [128], P(('gx', 'gy')), may hold values from 48 to 192
- block_order: int32 [256], replicated, may hold values from 0 to 255, each once
- sketch: bfloat16 [32768, 128], replicated, may hold values from -6 to 6
Outputs:
- cell_factor: bfloat16 [1048576, 128], P(('gx', 'gy'))
- gene_factor: float32 [32768, 128], P(('gx', 'gy'))
Inputs may be any that keep to these rules, and one draw needn't show every extreme that they name: On each device the live slots (those below its count) hold distinct coordinate pairs (tile_rows, tile_cols) in increasing lexicographic order; later slots are unused. `block_order`: device d along gx+gy owns the gene blocks in entries d * 2 to (d + 1) * 2 - 1.
All inputs are finite; a program needn't handle non-finite values.
Results may differ from a plain program's by a relative error of at most 0.0019.
Values sent between devices are 32-bit elements; how exact they have to be, the bound alone decides.
A program may use at most 192 MiB of HBM per device.

v0:
```python
import math

import jax
import jax.numpy as jnp
from jax import lax
from jax.sharding import PartitionSpec as P

TILE = 128
SKETCH = 128
GENES = 32768
CB_DEV = 64


def on_device(tiles, tile_rows, tile_cols, tile_counts, block_order, sketch):
    live_count = tile_counts[0]
    blocks_total = GENES // TILE
    sketch_blocks = sketch.reshape(blocks_total, TILE, SKETCH)
    width = 16
    turns = (live_count + width - 1) // width

    def take(start):
        tile_block = lax.dynamic_slice_in_dim(tiles, start, width, 0)
        row_block = lax.dynamic_slice_in_dim(tile_rows, start, width, 0)
        col_block = lax.dynamic_slice_in_dim(tile_cols, start, width, 0)
        alive = start + jnp.arange(width, dtype=jnp.int32) < live_count
        return (tile_block, row_block, col_block, alive)

    def cell_step(turn, total):
        tile_block, row_block, col_block, alive = take(turn * width)
        product = jnp.einsum(
            "tij,tjs->tis", tile_block, sketch_blocks[col_block], preferred_element_type=jnp.float32
        )
        product = jnp.where(alive[:, None, None], product, 0.0)
        return total.at[row_block].add(product)

    cell_sum = lax.fori_loop(0, turns, cell_step, jnp.zeros((CB_DEV, TILE, SKETCH), jnp.float32))
    cell_sum = cell_sum.reshape(CB_DEV * TILE, SKETCH)
    local_gram = jnp.dot(
        cell_sum.T, cell_sum, precision=lax.Precision.HIGHEST, preferred_element_type=jnp.float32
    )
    gram = lax.psum(local_gram, ("gx", "gy"))
    cells_all = CB_DEV * TILE * lax.axis_size("gx") * lax.axis_size("gy")
    lower = jnp.linalg.cholesky(gram)
    cell_factor = (
        math.sqrt(cells_all)
        * lax.linalg.triangular_solve(
            lower, cell_sum, left_side=False, lower=True, transpose_a=True
        )
    ).astype(jnp.bfloat16)
    cell_blocks = cell_factor.reshape(CB_DEV, TILE, SKETCH)

    def gene_step(turn, total):
        tile_block, row_block, col_block, alive = take(turn * width)
        product = jnp.einsum(
            "tji,tjs->tis", tile_block, cell_blocks[row_block], preferred_element_type=jnp.float32
        )
        product = jnp.where(alive[:, None, None], product, 0.0)
        return total.at[col_block].add(product)

    gene_sum = lax.fori_loop(
        0, turns, gene_step, jnp.zeros((blocks_total, TILE, SKETCH), jnp.float32)
    )
    ordered = gene_sum[block_order].reshape(GENES, SKETCH)
    owned = lax.psum_scatter(ordered, ("gx", "gy"), scatter_dimension=0, tiled=True)
    gene_gram = lax.psum(
        jnp.dot(
            owned.T, owned, precision=lax.Precision.HIGHEST, preferred_element_type=jnp.float32
        ),
        ("gx", "gy"),
    )
    lower_genes = jnp.linalg.cholesky(gene_gram)
    gene_factor = math.sqrt(GENES) * lax.linalg.triangular_solve(
        lower_genes, owned, left_side=False, lower=True, transpose_a=True
    )
    return (cell_factor, gene_factor)


def solution(mesh):
    placed = (
        P(("gx", "gy"), None, None),
        P(("gx", "gy")),
        P(("gx", "gy")),
        P(("gx", "gy")),
        P(),
        P(),
    )
    return jax.shard_map(
        on_device,
        mesh=mesh,
        in_specs=placed,
        out_specs=(P(("gx", "gy"), None), P(("gx", "gy"), None)),
        check_vma=False,
    )
```

profile of v0, /device:TPU:1, one launch (start us, length us, event | category | flops | bytes accessed | tf_op | source)
XLA Modules:
  0.0 1280.5 jit_solution(311369099258729333)
XLA Ops:
  7.9 2.4 broadcast_in_dim.44
  10.3 47.1 %while.20 = (s32[]{:T(128)}, f32[64,128,128]{2,1,0:T(8,128)}, s32[]{:T(128)}, s32[192]{0:T(256)S(1)}, s32[]{:T(128)}, /*index=5*/bf16[192,128,128]{2,1,0:T(8,128...) while((s32[]{:T(128)}, f32[64,128,128]{2,1,0:T(8,128)}, ...), condition=%wide.region_2.3_spmd, body=%wide.region_0.2_spmd.sunk | while | flops 67634312 | bytes 6296211 | solution.py:36
  10.4 4.0 gather_fusion
  14.5 0.7 add_compare_fusion.4
  15.1 1.3 convolution_select_fusion.4
  16.5 3.3 scatter_fusion
  19.9 4.0 gather_fusion
  23.9 0.7 add_compare_fusion.4
  24.6 1.3 convolution_select_fusion.4
  25.9 3.3 scatter_fusion
  29.3 4.0 gather_fusion
  33.4 0.7 add_compare_fusion.4
  34.0 1.3 convolution_select_fusion.4
  35.4 3.3 scatter_fusion
  38.8 4.0 gather_fusion
  42.8 0.7 add_compare_fusion.4
  43.5 1.3 convolution_select_fusion.4
  44.8 3.3 scatter_fusion
  48.2 4.0 gather_fusion
  52.2 0.7 add_compare_fusion.4
  52.9 1.3 convolution_select_fusion.4
  54.2 3.3 scatter_fusion
  57.5 10.8 convolution_bitcast_fusion
  68.6 208.5 %all-reduce.3.cloned.1.call-done = f32[128,128]{0,1:T(8,128)} async-done(((f32[128,128]{0,1:T(8,128)}), f32[128,128]{0,1:T(8,128)}) %all-reduce.3.cloned.1.call-update) | async-done | bytes 65552 | tf_op jit(solution)/shard_map/psum | solution.py:41
  277.2 0.9 copy.10
  278.1 0.9 fusion.10
  279.0 11.7 cholesky.44
  290.7 0.6 compare_reduce_fusion.1
  291.3 0.7 fusion.5
  292.0 9.8 custom-call.8
  301.8 6.1 fusion.4
  308.0 7.8 broadcast_in_dim.45
  315.8 39.0 %while.21 = (s32[]{:T(128)}, f32[256,128,128]{2,1,0:T(8,128)}, s32[]{:T(128)}, s32[192]{0:T(256)S(1)}, s32[]{:T(128)}, /*index=5*/bf16[192,128,128]{2,1,0:T(8,12...) while((s32[]{:T(128)}, f32[256,128,128]{2,1,0:T(8,128)}, ...), condition=%wide.region_8.10_spmd, body=%wide.region_6.9_spmd.sunk | while | flops 67634312 | bytes 6296211 | solution.py:60
  315.9 2.2 gather_fusion.1
  318.2 0.7 add_compare_fusion.5
  318.8 1.4 convolution_select_fusion.5
  320.2 3.4 scatter_fusion.1
  323.7 2.2 gather_fusion.1
  325.9 0.7 add_compare_fusion.5
  326.6 1.4 convolution_select_fusion.5
  328.0 3.4 scatter_fusion.1
  331.5 2.2 gather_fusion.1
  333.8 0.7 add_compare_fusion.5
  334.4 1.4 convolution_select_fusion.5
  335.8 3.4 scatter_fusion.1
  339.3 2.2 gather_fusion.1
  341.6 0.7 add_compare_fusion.5
  342.2 1.4 convolution_select_fusion.5
  343.6 3.4 scatter_fusion.1
  347.1 2.2 gather_fusion.1
  349.4 0.7 add_compare_fusion.5
  350.0 1.4 convolution_select_fusion.5
  351.5 3.4 scatter_fusion.1
  354.9 17.7 %gather_fusion.2 = f32[256,128,128]{2,1,0:T(8,128)} fusion(f32[256,128,128]{2,1,0:T(8,128)} %get-tuple-element.90, s32[1024]{0:T(1024)S(1)} %pad_clamp_fusion.2), kind=kCustom, calls=%fused_computation.2 | custom fusion | bytes 33555456 | tf_op jit(solution)/shard_map/gather | solution.py:63
  372.6 703.4 %reduce-scatter.2.cloned.1.call-done = f32[256,128]{1,0:T(8,128)} async-done(((f32[32768,128]{1,0:T(8,128)}), f32[256,128]{1,0:T(8,128)}) %reduce-scatter.2.cloned.1.call-update) | async-done | bytes 131088 | tf_op jit(solution)/shard_map/reduce_scatter | solution.py:64
  1076.0 2.0 fusion.11
  1078.0 169.5 %all-reduce.5.cloned.1.call-done = f32[128,128]{0,1:T(8,128)} async-done(((f32[128,128]{0,1:T(8,128)}), f32[128,128]{0,1:T(8,128)}) %all-reduce.5.cloned.1.call-update) | async-done | bytes 65552 | tf_op jit(solution)/shard_map/psum | solution.py:65
  1247.5 0.9 copy.13
  1248.4 0.9 fusion.8
  1249.3 11.7 cholesky.55
  1261.0 0.6 compare_reduce_fusion
  1261.7 0.7 fusion.6
  1262.3 9.8 custom-call.9
  1272.1 1.8 convolution_multiply_fusion.1
  (36 shorter events, 1.3 us)
Async XLA Ops:
  7.2 3.2 copy-start
  7.2 3.2 copy-start.1
  7.2 270.0 %all-reduce.3.cloned.1.call-start = ((), (), s32[]{:S(2)}) async-start(), calls=%async_computation.1 | async-start | bytes 131072 | tf_op jit(solution)/shard_map/psum | solution.py:41
  57.5 11.1 copy-start.2
  68.4 1007.6 %reduce-scatter.2.cloned.1.call-start = ((), (), s32[]{:S(2)}) async-start(), calls=%async_computation.2 | async-start | bytes 16908288 | tf_op jit(solution)/shard_map/reduce_scatter | solution.py:64
  372.5 874.9 %all-reduce.5.cloned.1.call-start = ((), (), s32[]{:S(2)}) async-start(), calls=%async_computation.3 | async-start | bytes 131072 | tf_op jit(solution)/shard_map/psum | solution.py:65
Sparse Core Ops, SparseCore 0:
  68.5 208.6 all-reduce.2
  372.7 703.2 reduce-scatter.1
  1081.3 166.1 all-reduce.4
where the time goes:
time: 1280 us
  waiting for transfers between devices  1080 us (84%)
  other arithmetic  88.4 us (7%)
  local copies, waits for them, and re-layouts  61.1 us (5%)
  matrix products  34.5 us (3%)
  between operations  14.5 us (1%)
    reduce_scatter x1, waiting for transfers between devices, on_device(): lax.psum_scatter(ordered, ('gx', 'gy'), scatter_dimension=0, tiled=True)  703 us
    psum x1, waiting for transfers between devices, on_device(): gram = lax.psum(local_gram, ('gx', 'gy'))  209 us
    psum x1, waiting for transfers between devices, on_device(): lax.psum(jnp.dot(owned.T, owned, precision=lax.Precision.HIGHEST, preferr...  169 us
  transfers between devices with their start and end apart: 3, of which 3 were waited for; matrix products, arithmetic and copies ran while one was open for 0% of the time, Pallas kernels for 0%

commit v1 on v0

v1 whole, which is shorter than its diff:
```python
import math

import jax
import jax.numpy as jnp
from jax import lax
from jax.experimental import pallas as pl
from jax.experimental.pallas import tpu as pltpu
from jax.sharding import PartitionSpec as P

TILE = 128
SKETCH = 128
GENES = 32768
CB_DEV = 64
BLOCKS = 256
SLOTS = 192
GROUP = 8
CHUNK = 16
F32 = jnp.float32
BF16 = jnp.bfloat16


def local_kernel(counts, rows, cols, order, tiles_hbm, sketch_hbm, split, w_out,
                 tiles, sketch, y_ref, place, tile_sems, sketch_sems):
    live = counts[0]
    w_ref = w_out.reshape(BLOCKS, TILE, SKETCH)
    n_tile = SLOTS // CHUNK
    n_sk = 4
    sk = GENES // n_sk

    def tile_copy(i):
        return pltpu.make_async_copy(
            tiles_hbm.at[pl.ds(i * CHUNK, CHUNK)], tiles.at[pl.ds(i * CHUNK, CHUNK)], tile_sems.at[i])

    def sketch_copy(i):
        return pltpu.make_async_copy(
            sketch_hbm.at[pl.ds(i * sk, sk)], sketch.at[pl.ds(i * sk, sk)], sketch_sems.at[i])

    for i in range(n_sk):
        sketch_copy(i).start()
    for i in range(n_tile):
        tile_copy(i).start()

    def invert(i, _):
        for u in range(8):
            place[order[i * 8 + u]] = i * 8 + u
        return 0
    lax.fori_loop(0, BLOCKS // 8, invert, 0)

    def clear_y(i, _):
        for u in range(4):
            y_ref[i * 4 + u] = jnp.zeros((TILE, SKETCH), F32)
        return 0
    lax.fori_loop(0, CB_DEV // 4, clear_y, 0)

    def clear_w(i, _):
        for u in range(4):
            w_ref[i * 4 + u] = jnp.zeros((TILE, SKETCH), F32)
        return 0
    lax.fori_loop(0, BLOCKS // 4, clear_w, 0)

    for i in range(n_sk):
        sketch_copy(i).wait()

    def cells(i):
        base = i * GROUP
        parts = []
        for u in range(GROUP):
            c = pl.multiple_of(cols[base + u] * TILE, TILE)
            p = jnp.dot(tiles[base + u], sketch[pl.ds(c, TILE), :], preferred_element_type=F32)
            parts.append(jnp.where(base + u < live, p, 0.0))
        for u in range(GROUP):
            r = rows[base + u]
            y_ref[r] = y_ref[r] + parts[u]

    for i in range(n_tile):
        tile_copy(i).wait()

    def cell_body(i, _):
        cells(i)
        return 0
    steps = (live + GROUP - 1) // GROUP
    lax.fori_loop(0, steps, cell_body, 0)

    def cut(i, _):
        for u in range(4):
            v = y_ref[i * 4 + u]
            hi = v.astype(BF16)
            split[i * 4 + u, :, :SKETCH] = hi
            split[i * 4 + u, :, SKETCH:] = (v - hi.astype(F32)).astype(BF16)
        return 0
    lax.fori_loop(0, CB_DEV // 4, cut, 0)

    def gene_body(i, _):
        base = i * GROUP
        parts = []
        for u in range(GROUP):
            r = rows[base + u]
            p = lax.dot_general(tiles[base + u], split[r], (((0,), (0,)), ((), ())),
                                preferred_element_type=F32)
            v = p[:, :SKETCH] + p[:, SKETCH:]
            parts.append(jnp.where(base + u < live, v, 0.0))
        for u in range(GROUP):
            o = place[cols[base + u]]
            w_ref[o] = w_ref[o] + parts[u]
        return 0
    lax.fori_loop(0, steps, gene_body, 0)


def local_pass(tiles, rows, cols, counts, order, sketch):
    smem = pl.BlockSpec(memory_space=pltpu.SMEM)
    anyp = pl.BlockSpec(memory_space=pl.ANY)
    vmem = pl.BlockSpec(memory_space=pltpu.VMEM)
    return pl.pallas_call(
        local_kernel,
        name="local_pass",
        out_shape=(
            pltpu.VMEM((CB_DEV, TILE, 2 * SKETCH), BF16),
            pltpu.VMEM((4, 2, 4, 4, 2 * TILE, SKETCH), F32),
        ),
        in_specs=[smem, smem, smem, smem, anyp, anyp],
        out_specs=(vmem, vmem),
        scratch_shapes=[
            pltpu.VMEM((SLOTS, TILE, TILE), BF16),
            pltpu.VMEM((GENES, SKETCH), BF16),
            pltpu.VMEM((CB_DEV, TILE, SKETCH), F32),
            pltpu.SMEM((BLOCKS,), jnp.int32),
            pltpu.SemaphoreType.DMA((SLOTS // CHUNK,)),
            pltpu.SemaphoreType.DMA((4,)),
        ],
        compiler_params=pltpu.CompilerParams(vmem_limit_bytes=24 << 20),
    )(counts, rows, cols, order, tiles, sketch)


PARTS = ((0, 88), (88, 88), (176, 80))
ORDERS = ((2, 1, 0), (1, 0, 2), (0, 2, 1))
MESH = pl.DeviceIdType.MESH
HIGH = lax.Precision.HIGHEST


def cut_two(v):
    hi = v.astype(BF16)
    return hi, (v - hi.astype(F32)).astype(BF16)


def inverse_factor(gram, work, out):
    work[:, :SKETCH] = gram[...]
    ri = lax.broadcasted_iota(jnp.int32, (SKETCH, SKETCH), 0)
    ci = lax.broadcasted_iota(jnp.int32, (SKETCH, SKETCH), 1)
    work[:, SKETCH:] = jnp.where(ri == ci, 1.0, 0.0)
    lane = lax.broadcasted_iota(jnp.int32, (1, SKETCH), 1)
    down = lax.broadcasted_iota(jnp.int32, (SKETCH, 1), 0)

    def body(j, carry):
        row = work[pl.ds(j, 1), :]
        left = work[:, :SKETCH]
        pivot = jnp.sum(jnp.where(lane == j, row[:, :SKETCH], 0.0), axis=1, keepdims=True)
        col = jnp.sum(jnp.where(ci == j, left, 0.0), axis=1, keepdims=True)
        mult = jnp.where(down > j, col, 0.0)
        scaled = row / pivot
        work[:, :SKETCH] = left - mult * scaled[:, :SKETCH]
        work[:, SKETCH:] = work[:, SKETCH:] - mult * scaled[:, SKETCH:]
        return carry

    lax.fori_loop(0, SKETCH, body, 0)
    diag = jnp.sum(jnp.where(ri == ci, work[:, :SKETCH], 0.0), axis=1, keepdims=True)
    out[...] = work[:, SKETCH:] / jnp.sqrt(diag)


def exchange_kernel(split, w, cell_out, gene_out,
                    acc, box1, box2, box3, cell, gram, total, work, inv1, inv2, zed,
                    cur, first, slots,
                    in_send, in_recv, ring_send, ring_recv, sum_send, sum_recv, out_sem):
    gx = lax.axis_index("gx")
    gy = lax.axis_index("gy")
    z, core = gx // 2, gx % 2
    y, x = gy // 4, gy % 4
    me = (z, y, x)

    def device(pos, c):
        return (pos[0] * 2 + c, pos[1] * 4 + pos[2])

    def moved(axis, k):
        pos = list(me)
        pos[axis] = (pos[axis] + k + 4) % 4
        return pos

    partner = device(me, 1 - core)
    barrier = pltpu.get_barrier_semaphore()
    peers = [partner] + [device(moved(a, k), core) for a in range(3) for k in (1, 2, 3)]
    for peer in peers:
        pl.semaphore_signal(barrier, inc=1, device_id=peer, device_id_type=MESH)
    pl.semaphore_wait(barrier, len(peers))

    def remote(src, dst, send, recv, peer):
        return pltpu.make_async_remote_copy(
            src_ref=src, dst_ref=dst, send_sem=send, recv_sem=recv,
            device_id=peer, device_id_type=MESH)

    def at(fixed, part, halves=None, rows=None):
        idx = [fixed.get(d, slice(None)) for d in range(3)]
        free = [d for d in range(3) if d not in fixed]
        if halves is not None and free:
            idx[free[0]] = pl.ds(2 * halves, 2)
        r0, nr = PARTS[part]
        if rows is not None:
            r0, nr = r0 + rows[0], rows[1]
        idx.append(pl.ds(r0, nr))
        return tuple(idx)

    def add(dst, src, lead):
        if len(lead) == 2:
            n = lead[1]

            def body(i, carry):
                a, b = i // n, i % n
                dst[a, b] = dst[a, b] + src[a, b]
                return carry
            lax.fori_loop(0, lead[0] * n, body, 0)
        elif len(lead) == 1:
            def body1(i, carry):
                dst[i] = dst[i] + src[i]
                return carry
            lax.fori_loop(0, lead[0], body1, 0)
        else:
            dst[...] = dst[...] + src[...]

    def with_core(idx, c):
        return (idx[0], c) + tuple(idx[1:])

    steps = (2, 1, 3, 0)
    pieces = {}
    for n, k in enumerate(steps):
        for p in range(3):
            a = ORDERS[p][0]
            idx = at({a: (me[a] + k) % 4}, p)
            copy = remote(w.at[with_core(idx, 1 - core)], acc.at[idx],
                          in_send.at[n * 3 + p], in_recv.at[n * 3 + p], partner)
            copy.start()
            pieces[k, p] = copy, idx

    def gram_body(i, g):
        v = split[pl.ds(i * 8, 8)].reshape(8 * TILE, 2 * SKETCH)
        return g + lax.dot_general(v, v, (((0,), (0,)), ((), ())), preferred_element_type=F32)
    g = lax.fori_loop(0, CB_DEV // 8, gram_body, jnp.zeros((2 * SKETCH, 2 * SKETCH), F32))
    gram[...] = (g[:SKETCH, :SKETCH] + g[SKETCH:, SKETCH:]) + (g[:SKETCH, SKETCH:] + g[SKETCH:, :SKETCH])

    half = SKETCH // 2

    def sum_start(w_):
        copy = remote(gram.at[pl.ds((1 - core) * half, half)], first.at[w_],
                      sum_send.at[w_, 9], sum_recv.at[w_, 9], partner)
        copy.start()
        return copy

    def sum_send_axis(w_, a, value):
        cur[w_, a] = value
        slots[w_, a, me[a]] = value
        copies = []
        for k in (1, 2, 3):
            copy = remote(cur.at[w_, a], slots.at[w_, a, me[a]],
                          sum_send.at[w_, a * 3 + k - 1], sum_recv.at[w_, a * 3 + k - 1],
                          device(moved(a, k), core))
            copy.start()
            copies.append(copy)
        return copies

    def sum_axis(w_, a, copies):
        for copy in copies:
            copy.wait()
        return (slots[w_, a, 0] + slots[w_, a, 1]) + (slots[w_, a, 2] + slots[w_, a, 3])

    def sum_first(w_, copy):
        copy.wait()
        return gram[pl.ds(core * half, half), :] + first[w_]

    def sum_last(w_, value):
        mine = pl.ds(core * half, half)
        cur[w_, 3] = value
        total[w_, mine, :] = value
        copy = remote(cur.at[w_, 3], total.at[w_, mine], sum_send.at[w_, 10], sum_recv.at[w_, 10], partner)
        copy.start()
        return copy

    g0 = sum_start(0)

    HALF_ROWS = ((0, 48), (48, None))
    boxes = (box1, box2, box3)
    fixed = [dict() for _ in range(3)]

    def span(phase, p, h):
        nr = PARTS[p][1]
        if phase < 2:
            return None, nr
        return ((0, 48), 48) if h == 0 else ((48, nr - 48), nr - 48)

    def view(phase, p, coord, h):
        f = dict(fixed[p])
        f[ORDERS[p][phase]] = coord
        rows, nr = span(phase, p, h)
        return acc.at[at(f, p, h, rows)]

    def box(phase, p, m, h):
        nr = span(phase, p, h)[1]
        b = boxes[phase]
        if phase == 0:
            return b.at[p, m, :, :, pl.ds(0, nr)]
        if phase == 1:
            return b.at[p, m, :, pl.ds(0, nr)]
        return b.at[p, m, pl.ds(0, nr)]

    leads = ((2, 4), (2,), ())

    def send(phase, p, m):
        a = ORDERS[p][phase]
        sign = 1 if m % 2 == 0 else -1
        coord = (me[a] + (2 if m < 2 else sign) + 4) % 4
        h = (0, 1, 1, 0, 0, 1)[m]
        copy = remote(view(phase, p, coord, h), box(phase, p, m, h),
                      ring_send.at[phase, p * 6 + m], ring_recv.at[phase, p * 6 + m],
                      device(moved(a, sign), core))
        copy.start()
        return copy

    def pass_on(phase, p, m, copy):
        a = ORDERS[p][phase]
        sign = 1 if m % 2 == 0 else -1
        h = m % 2
        copy.wait_recv()
        add(view(phase, p, (me[a] + sign + 4) % 4, h), box(phase, p, m, h), leads[phase])

    def land(phase, p, m, copy):
        a = ORDERS[p][phase]
        h = (0, 1, 1, 0, 0, 1)[m]
        copy.wait_recv()
        add(view(phase, p, me[a], h), box(phase, p, m, h), leads[phase])

    def merge(k, p):
        copy, idx = pieces[k, p]
        copy.wait()
        add(acc.at[idx], w.at[with_core(idx, core)], (4, 4))

    ring = {}
    for p in range(3):
        merge(2, p)
        ring[0, p, 0] = send(0, p, 0)
        ring[0, p, 1] = send(0, p, 1)
    gx_ = sum_send_axis(0, 2, sum_first(0, g0))
    for p in range(3):
        merge(1, p)
        ring[0, p, 2] = send(0, p, 2)
        merge(3, p)
        ring[0, p, 3] = send(0, p, 3)
    gy_ = sum_send_axis(0, 1, sum_axis(0, 2, gx_))
    for p in range(3):
        for m in (0, 1):
            pass_on(0, p, m, ring[0, p, m])
            ring[0, p, 4 + m] = send(0, p, 4 + m)
    gz_ = sum_send_axis(0, 0, sum_axis(0, 1, gy_))
    for p in range(3):
        merge(0, p)
    gl_ = sum_last(0, sum_axis(0, 0, gz_))
    gl_.wait()

    inverse_factor(total.at[0], work, inv1)
    lh, ll = cut_two(inv1[...] * math.sqrt(CB_DEV * TILE * 128))
    weights = jnp.concatenate(
        [jnp.concatenate([lh, lh], axis=1), jnp.concatenate([ll, jnp.zeros_like(ll)], axis=1)], axis=0)

    def cell_body(i, carry):
        v = split[pl.ds(i * 4, 4)].reshape(4 * TILE, 2 * SKETCH)
        o = lax.dot_general(v, weights, (((1,), (1,)), ((), ())), preferred_element_type=F32)
        cell[pl.ds(pl.multiple_of(i * 4 * TILE, 4 * TILE), 4 * TILE), :] = (
            o[:, :SKETCH] + o[:, SKETCH:]).astype(BF16)
        return carry
    lax.fori_loop(0, CB_DEV // 4, cell_body, 0)
    out_copy = pltpu.make_async_copy(cell, cell_out, out_sem.at[0])
    out_copy.start()

    for phase in range(3):
        if phase:
            for p in range(3):
                for m in range(4):
                    ring[phase, p, m] = send(phase, p, m)
            for p in range(3):
                for m in (0, 1):
                    pass_on(phase, p, m, ring[phase, p, m])
                    ring[phase, p, 4 + m] = send(phase, p, 4 + m)
        for m in (2, 3, 4, 5):
            for p in range(3):
                land(phase, p, m, ring[phase, p, m])
        for p in range(3):
            for m in range(6):
                ring[phase, p, m].wait_send()
            fixed[p][ORDERS[p][phase]] = me[ORDERS[p][phase]]

    own = acc[z, y, x]
    zv = lax.dot_general(own, inv1[...], (((1,), (1,)), ((), ())), precision=HIGH, preferred_element_type=F32)
    zed[...] = zv
    gram[...] = lax.dot_general(zv, zv, (((0,), (0,)), ((), ())), precision=HIGH, preferred_element_type=F32)
    value = sum_first(1, sum_start(1))
    for a in (2, 1, 0):
        value = sum_axis(1, a, sum_send_axis(1, a, value))
    sum_last(1, value).wait()
    inverse_factor(total.at[1], work, inv2)
    gene_out[...] = math.sqrt(GENES) * lax.dot_general(
        zed[...], inv2[...], (((1,), (1,)), ((), ())), precision=HIGH, preferred_element_type=F32)
    out_copy.wait()


def exchange(split, w):
    vmem = pl.BlockSpec(memory_space=pltpu.VMEM)
    sq = (SKETCH, SKETCH)
    return pl.pallas_call(
        exchange_kernel,
        name="exchange",
        out_shape=(
            jax.ShapeDtypeStruct((CB_DEV * TILE, SKETCH), BF16),
            jax.ShapeDtypeStruct((2 * TILE, SKETCH), F32),
        ),
        in_specs=[vmem, vmem],
        out_specs=(pl.BlockSpec(memory_space=pl.ANY), vmem),
        scratch_shapes=[
            pltpu.VMEM((4, 4, 4, 2 * TILE, SKETCH), F32),
            pltpu.VMEM((3, 6, 2, 4, 88, SKETCH), F32),
            pltpu.VMEM((3, 6, 2, 88, SKETCH), F32),
            pltpu.VMEM((3, 6, 48, SKETCH), F32),
            pltpu.VMEM((CB_DEV * TILE, SKETCH), BF16),
            pltpu.VMEM(sq, F32),
            pltpu.VMEM((2,) + sq, F32),
            pltpu.VMEM((SKETCH, 2 * SKETCH), F32),
            pltpu.VMEM(sq, F32),
            pltpu.VMEM(sq, F32),
            pltpu.VMEM((2 * TILE, SKETCH), F32),
            pltpu.VMEM((2, 4, SKETCH // 2, SKETCH), F32),
            pltpu.VMEM((2, SKETCH // 2, SKETCH), F32),
            pltpu.VMEM((2, 3, 4, SKETCH // 2, SKETCH), F32),
            pltpu.SemaphoreType.DMA((12,)),
            pltpu.SemaphoreType.DMA((12,)),
            pltpu.SemaphoreType.DMA((3, 18)),
            pltpu.SemaphoreType.DMA((3, 18)),
            pltpu.SemaphoreType.DMA((2, 11)),
            pltpu.SemaphoreType.DMA((2, 11)),
            pltpu.SemaphoreType.DMA((1,)),
        ],
        compiler_params=pltpu.CompilerParams(
            collective_id=0, has_side_effects=True, vmem_limit_bytes=26 << 20),
    )(pltpu.with_memory_space_constraint(split, pltpu.VMEM), pltpu.with_memory_space_constraint(w, pltpu.VMEM))


def on_device(tiles, tile_rows, tile_cols, tile_counts, block_order, sketch):
    split, w = local_pass(tiles, tile_rows, tile_cols, tile_counts, block_order, sketch)
    return exchange(split, w)


def solution(mesh):
    placed = (
        P(("gx", "gy"), None, None),
        P(("gx", "gy")),
        P(("gx", "gy")),
        P(("gx", "gy")),
        P(),
        P(),
    )
    return jax.shard_map(
        on_device,
        mesh=mesh,
        in_specs=placed,
        out_specs=(P(("gx", "gy"), None), P(("gx", "gy"), None)),
        check_vma=False,
    )
```

time: 1280 us -> 145 us (0.11)
  waiting for transfers between devices: 1080 us -> 0 us
  Pallas kernels: 0 us -> 125 us
  other arithmetic: 88.4 us -> 0 us
  local copies, waits for them, and re-layouts: 61.1 us -> 18.3 us
  matrix products: 34.5 us -> 0 us
  between operations: 14.5 us -> 1.31 us
    reduce_scatter x1 -> x0, waiting for transfers between devices: 703 us -> none  [on_device(): lax.psum_scatter(ordered, ('gx', 'gy'), scatter_dimension=0, tiled=True)]
    psum x2 -> x0, waiting for transfers between devices: 378 us -> none  [the longest x1 209 us: on_device(): gram = lax.psum(local_gram, ('gx', 'gy'))]
    pallas_call x0 -> x2, Pallas kernels: none -> 125 us  [the longest x1 113 us: exchange(): pl.pallas_call(exchange_kernel, name='exchange', out_shape=(jax.ShapeDtyp...]
    gather x11 -> x0, local copies, waits for them, and re-layouts: 49 us -> none  [the longest x5 20.1 us: cell_step(): sketch_blocks[col_block]]
    another operation x10 -> x0, other arithmetic: 45.7 us -> none  [the longest x3 12.4 us: on_device(): lower = jnp.linalg.cholesky(gram)]
    scatter-add x10 -> x0, other arithmetic: 33.6 us -> none  [the longest x5 17.1 us: gene_step(): return total.at[col_block].add(product)]
    dot_general x12 -> x0, matrix products: 26.5 us -> none  [the longest x1 10.8 us: on_device(): jnp.dot(cell_sum.T, cell_sum, precision=lax.Precision.HIGHEST, preferred_...]
    unnamed x6 -> x14, local copies, waits for them, and re-layouts: 0.01 us -> 18.3 us
  transfers between devices with their start and end apart: 3 -> 0, of which waited for: 3 -> 0; matrix products, arithmetic and copies ran while one was open for 0% -> 0% of each run, Pallas kernels for 0% -> 0%
where the time goes in v1:
time: 145 us
  Pallas kernels  125 us (86%)
  local copies, waits for them, and re-layouts  18.3 us (13%)
    pallas_call x1, Pallas kernels, exchange(): pl.pallas_call(exchange_kernel, name='exchange', out_shape=(jax.ShapeDtyp...  113 us
    unnamed x14, local copies, waits for them, and re-layouts  18.3 us
    pallas_call x1, Pallas kernels, local_pass(): pl.pallas_call(local_kernel, name='local_pass', out_shape=(pltpu.VMEM((CB...  11.8 us

profile of v1, /device:TPU:1, one launch (start us, length us, event | category | flops | bytes accessed | tf_op | source)
XLA Modules:
  0.0 144.8 jit_solution(17948344555119021036)
XLA Ops:
  1.3 0.0 copy-start.2
  1.3 2.8 %copy-done.2 = bf16[192,128,128]{2,1,0:T(8,128)(2,1)S(1)} copy-done((bf16[192,128,128]{2,1,0:T(8,128)(2,1)S(1)}, bf16[192,128,128]{2,1,0:T(8,128)(2,1)}, u32[]{:S(2)}) %copy-start.2) | copy-done | bytes 6291480
  4.1 0.0 copy-start.3
  4.1 0.7 copy-done.3
  4.7 0.0 copy-start.4
  4.7 0.7 copy-done.4
  5.4 0.0 copy-start.5
  5.4 0.7 copy-done.5
  6.1 11.8 %local_pass.1 = (bf16[64,128,256]{2,1,0:T(8,128)(2,1)S(1)}, f32[4,2,4,4,256,128]{5,4,3,2,1,0:T(8,128)S(1)}) custom-call(s32[1]{0:T(128)S(6)} %copy.10.counts, s32[192]{0:T(256)S(1)} %copy-done.3, s32[192]{0:T(256)S(1)} %copy-done.4, s32[256]{0:T(256)S(1)} %copy-done.5, bf16[192,128,128]{2,1,0:T(8,128)(2,1)S(1)} %copy-done.2, bf16[32768,128]{1,0:T(8,128)(2,1)} %sketch_hbm.1), custom_call_target="tpu_custom_call" | custom-call | tf_op jit(solution)/shard_map/local_pass/pallas_call | solution.py:113
  17.9 0.0 copy-start
  18.0 5.7 %copy-done = f32[4,2,4,4,256,128]{5,4,3,2,1,0:T(8,128)} copy-done((f32[4,2,4,4,256,128]{5,4,3,2,1,0:T(8,128)}, f32[4,2,4,4,256,128]{5,4,3,2,1,0:T(8,128)S(1)}, u32[]{:S(2)}) %copy-start) | copy-done | bytes 16777240
  23.7 0.0 copy-start.1
  23.7 5.8 %copy-done.1 = f32[4,2,4,4,256,128]{5,4,3,2,1,0:T(8,128)S(1)} copy-done((f32[4,2,4,4,256,128]{5,4,3,2,1,0:T(8,128)S(1)}, f32[4,2,4,4,256,128]{5,4,3,2,1,0:T(8,128)}, u32[]{:S(2)}) %copy-start.1) | copy-done | bytes 16777240
  29.4 113.4 %exchange.1 = (bf16[8192,128]{1,0:T(8,128)(2,1)S(1)}, f32[256,128]{1,0:T(8,128)S(1)}) custom-call(bf16[64,128,256]{2,1,0:T(8,128)(2,1)S(1)} %get-tuple-element.4.split, f32[4,2,4,4,256,128]{5,4,3,2,1,0:T(8,128)S(1)} %copy-done.1), custom_call_target="tpu_custom_call" | custom-call | tf_op jit(solution)/shard_map/exchange/pallas_call | solution.py:413
  142.9 1.3 copy.11
  144.2 0.7 copy.12
Async XLA Ops:
  1.3 2.8 %copy-start.2 = (bf16[192,128,128]{2,1,0:T(8,128)(2,1)S(1)}, bf16[192,128,128]{2,1,0:T(8,128)(2,1)}, u32[]{:S(2)}) copy-start(bf16[192,128,128]{2,1,0:T(8,128)(2,1)} %tiles_hbm.1) | copy-start | bytes 18874372
  4.1 0.7 copy-start.3
  4.7 0.7 copy-start.4
  5.4 0.7 copy-start.5
  17.9 5.7 %copy-start = (f32[4,2,4,4,256,128]{5,4,3,2,1,0:T(8,128)}, f32[4,2,4,4,256,128]{5,4,3,2,1,0:T(8,128)S(1)}, u32[]{:S(2)}) copy-start(f32[4,2,4,4,256,128]{5,4,3,2,1,0:T(8,128)S(1)} %get-tuple-element.5.w) | copy-start | bytes 50331652
  23.7 5.8 %copy-start.1 = (f32[4,2,4,4,256,128]{5,4,3,2,1,0:T(8,128)S(1)}, f32[4,2,4,4,256,128]{5,4,3,2,1,0:T(8,128)}, u32[]{:S(2)}) copy-start(f32[4,2,4,4,256,128]{5,4,3,2,1,0:T(8,128)} %copy-done) | copy-start | bytes 50331652

commit v2 on v1

v2 whole, which is shorter than its diff:
```python
import math

import jax
import jax.numpy as jnp
from jax import lax
from jax.experimental import pallas as pl
from jax.experimental.pallas import tpu as pltpu
from jax.sharding import PartitionSpec as P

TILE = 128
SKETCH = 128
GENES = 32768
CB_DEV = 64
BLOCKS = 256
SLOTS = 192
GROUP = 8
CHUNK = 16
F32 = jnp.float32
BF16 = jnp.bfloat16


def local_kernel(counts, rows_hbm, cols_hbm, order_hbm, tiles_hbm, sketch_hbm, split, w_out,
                 tiles, sketch, y_ref, place, rows, cols, order,
                 tile_sems, sketch_sems, index_sems):
    lists = ((rows_hbm, rows), (cols_hbm, cols), (order_hbm, order))
    index_copies = [pltpu.make_async_copy(a, b, index_sems.at[i]) for i, (a, b) in enumerate(lists)]
    for copy in index_copies:
        copy.start()
    w_ref = w_out.reshape(BLOCKS, TILE, SKETCH)
    n_tile = SLOTS // CHUNK
    n_sk = 4
    sk = GENES // n_sk

    def tile_copy(i):
        return pltpu.make_async_copy(
            tiles_hbm.at[pl.ds(i * CHUNK, CHUNK)], tiles.at[pl.ds(i * CHUNK, CHUNK)], tile_sems.at[i])

    def sketch_copy(i):
        return pltpu.make_async_copy(
            sketch_hbm.at[pl.ds(i * sk, sk)], sketch.at[pl.ds(i * sk, sk)], sketch_sems.at[i])

    for i in range(n_sk):
        sketch_copy(i).start()
    for i in range(n_tile):
        tile_copy(i).start()

    for copy in index_copies:
        copy.wait()
    live = counts[0]

    def invert(i, _):
        for u in range(8):
            place[order[i * 8 + u]] = i * 8 + u
        return 0
    lax.fori_loop(0, BLOCKS // 8, invert, 0)

    def clear_y(i, _):
        for u in range(4):
            y_ref[i * 4 + u] = jnp.zeros((TILE, SKETCH), F32)
        return 0
    lax.fori_loop(0, CB_DEV // 4, clear_y, 0)

    def clear_w(i, _):
        for u in range(4):
            w_ref[i * 4 + u] = jnp.zeros((TILE, SKETCH), F32)
        return 0
    lax.fori_loop(0, BLOCKS // 4, clear_w, 0)

    for i in range(n_sk):
        sketch_copy(i).wait()

    def cells(i):
        base = i * GROUP
        parts = []
        for u in range(GROUP):
            c = pl.multiple_of(cols[base + u] * TILE, TILE)
            p = jnp.dot(tiles[base + u], sketch[pl.ds(c, TILE), :], preferred_element_type=F32)
            parts.append(jnp.where(base + u < live, p, 0.0))
        for u in range(GROUP):
            r = rows[base + u]
            y_ref[r] = y_ref[r] + parts[u]

    def cell_body(i, _):
        @pl.when(i % (CHUNK // GROUP) == 0)
        def _():
            tile_copy(i // (CHUNK // GROUP)).wait()
        cells(i)
        return 0
    steps = (live + GROUP - 1) // GROUP
    lax.fori_loop(0, steps, cell_body, 0)

    def late(i, _):
        tile_copy(i).wait()
        return 0
    lax.fori_loop((live + CHUNK - 1) // CHUNK, n_tile, late, 0)

    def cut(i, _):
        for u in range(4):
            v = y_ref[i * 4 + u]
            hi = v.astype(BF16)
            split[i * 4 + u, :, :SKETCH] = hi
            split[i * 4 + u, :, SKETCH:] = (v - hi.astype(F32)).astype(BF16)
        return 0
    lax.fori_loop(0, CB_DEV // 4, cut, 0)

    def gene_body(i, _):
        base = i * GROUP
        parts = []
        for u in range(GROUP):
            r = rows[base + u]
            p = lax.dot_general(tiles[base + u], split[r], (((0,), (0,)), ((), ())),
                                preferred_element_type=F32)
            v = p[:, :SKETCH] + p[:, SKETCH:]
            parts.append(jnp.where(base + u < live, v, 0.0))
        for u in range(GROUP):
            o = place[cols[base + u]]
            w_ref[o] = w_ref[o] + parts[u]
        return 0
    lax.fori_loop(0, steps, gene_body, 0)


def local_pass(tiles, rows, cols, counts, order, sketch):
    hbm = [pltpu.with_memory_space_constraint(v, pltpu.HBM) for v in (rows, cols, order, tiles, sketch)]
    anyp = pl.BlockSpec(memory_space=pl.ANY)
    vmem = pl.BlockSpec(memory_space=pltpu.VMEM)
    return pl.pallas_call(
        local_kernel,
        name="local_pass",
        out_shape=(
            pltpu.VMEM((CB_DEV, TILE, 2 * SKETCH), BF16),
            pltpu.VMEM((4, 2, 4, 4, 2 * TILE, SKETCH), F32),
        ),
        in_specs=[pl.BlockSpec(memory_space=pltpu.SMEM)] + [anyp] * 5,
        out_specs=(vmem, vmem),
        scratch_shapes=[
            pltpu.VMEM((SLOTS, TILE, TILE), BF16),
            pltpu.VMEM((GENES, SKETCH), BF16),
            pltpu.VMEM((CB_DEV, TILE, SKETCH), F32),
            pltpu.SMEM((BLOCKS,), jnp.int32),
            pltpu.SMEM((SLOTS,), jnp.int32),
            pltpu.SMEM((SLOTS,), jnp.int32),
            pltpu.SMEM((BLOCKS,), jnp.int32),
            pltpu.SemaphoreType.DMA((SLOTS // CHUNK,)),
            pltpu.SemaphoreType.DMA((4,)),
            pltpu.SemaphoreType.DMA((4,)),
        ],
        compiler_params=pltpu.CompilerParams(vmem_limit_bytes=26 << 20),
    )(counts, *hbm)


PARTS = ((0, 88), (88, 88), (176, 80))
ORDERS = ((2, 1, 0), (1, 0, 2), (0, 2, 1))
ROUNDS = (2, 1, 3, 0)
TURN = (0, 1, 1, 0, 0, 1)
MESH = pl.DeviceIdType.MESH
HIGH = lax.Precision.HIGHEST


def cut_two(v):
    hi = v.astype(BF16)
    return hi, (v - hi.astype(F32)).astype(BF16)


WINDOW = 4


def factor_start(gram, work):
    work[:, :SKETCH] = gram[...]
    ri = lax.broadcasted_iota(jnp.int32, (SKETCH, SKETCH), 0)
    ci = lax.broadcasted_iota(jnp.int32, (SKETCH, SKETCH), 1)
    work[:, SKETCH:] = jnp.where(ri == ci, 1.0, 0.0)


def factor_steps(work, out, first, last):
    rows = 32
    down = lax.broadcasted_iota(jnp.int32, (rows, 1), 0)

    def lane(v, n):
        return jnp.broadcast_to(v[:, n:n + 1], (v.shape[0], SKETCH))

    def group(j, l0):
        tile = pl.ds(pl.multiple_of(j, 8), 8)
        lt = work[tile, :SKETCH]
        rt = work[tile, SKETCH:]
        left = [jnp.broadcast_to(lt[l0 + t:l0 + t + 1], (8, SKETCH)) for t in range(WINDOW)]
        right = [jnp.broadcast_to(rt[l0 + t:l0 + t + 1], (8, SKETCH)) for t in range(WINDOW)]
        e = {(s, t): lane(left[s], l0 + t) for s in range(WINDOW) for t in range(s, WINDOW)}
        w = {}
        inv = []
        for s in range(WINDOW):
            inv.append(1.0 / e[s, s])
            for t in range(s + 1, WINDOW):
                w[s, t] = e[s, t] * inv[s]
            for t in range(s + 1, WINDOW):
                for u in range(t, WINDOW):
                    e[t, u] = e[t, u] - w[s, t] * e[s, u]
                left[t] = left[t] - w[s, t] * left[s]
                right[t] = right[t] - w[s, t] * right[s]
        done = [right[t] * (1.0 / jnp.sqrt(e[t, t])) for t in range(WINDOW)]
        ql = [(left[t] * inv[t])[:1] for t in range(WINDOW)]
        qr = [(right[t] * inv[t])[:1] for t in range(WINDOW)]
        ww = {k: v[:1] for k, v in w.items()}
        for i in range(SKETCH // rows):
            here = pl.ds(i * rows, rows)
            a = work[here, :SKETCH]
            b = work[here, SKETCH:]
            below = down + i * rows > j + l0 + WINDOW - 1
            c = [jnp.where(below, lane(a, l0 + t), 0.0) for t in range(WINDOW)]
            for t in range(1, WINDOW):
                for s in range(t):
                    c[t] = c[t] - c[s] * ww[s, t]
            for t in range(WINDOW):
                a = a - c[t] * ql[t]
                b = b - c[t] * qr[t]
            if l0 + WINDOW == 8:
                a = pltpu.roll(a, SKETCH - 8, 1)
            work[here, :SKETCH] = a
            work[here, SKETCH:] = b
        return done

    sub = lax.broadcasted_iota(jnp.int32, (8, 1), 0)

    def body(i, carry):
        done = []
        for l0 in range(0, 8, WINDOW):
            done += group(i * 8, l0)
        tile = done[0]
        for t in range(1, 8):
            tile = jnp.where(sub == t, done[t], tile)
        out[pl.ds(pl.multiple_of(i * 8, 8), 8), :] = tile
        return carry

    lax.fori_loop(first, last, body, 0)


def exchange_kernel(split, w, cell_out, gene_out,
                    acc, box1, box2, box3, cell, gram, total, work, inv1, inv2, zed,
                    cur, first, slots,
                    in_send, in_recv, ring_send, ring_recv, sum_send, sum_recv, out_sem):
    gx = lax.axis_index("gx")
    gy = lax.axis_index("gy")
    z, core = gx // 2, gx % 2
    y, x = gy // 4, gy % 4
    me = (z, y, x)

    def device(pos, c):
        return (pos[0] * 2 + c, pos[1] * 4 + pos[2])

    def around(axis, k):
        return (me[axis] + k + 4) % 4

    def moved(axis, k):
        pos = list(me)
        pos[axis] = around(axis, k)
        return pos

    near = [(dx, dc) for dx in range(4) for dc in range(2) if dx or dc]

    def near_device(dx, dc):
        return device(moved(2, dx), 1 - core if dc else core)

    partner = near_device(0, 1)
    barrier = pltpu.get_barrier_semaphore()
    peers = [near_device(dx, dc) for dx, dc in near]
    peers += [device(moved(a, k), core) for a in (0, 1) for k in (1, 2, 3)]
    for peer in peers:
        pl.semaphore_signal(barrier, inc=1, device_id=peer, device_id_type=MESH)
    pl.semaphore_wait(barrier, len(peers))

    sends = []

    def remote(src, dst, send, recv, peer):
        copy = pltpu.make_async_remote_copy(
            src_ref=src, dst_ref=dst, send_sem=send, recv_sem=recv,
            device_id=peer, device_id_type=MESH)
        copy.start()
        sends.append(copy)
        return copy

    def add(dst, src, lead):
        if lead:
            def body(i, carry):
                dst[i] = dst[i] + src[i]
                return carry
            lax.fori_loop(0, lead, body, 0)
        else:
            dst[...] = dst[...] + src[...]

    def place(p, ca, cb, cc, rows=None):
        idx = [None] * 3
        for d, v in zip(ORDERS[p], (ca, cb, cc)):
            idx[d] = v
        r0, nr = PARTS[p]
        if rows is not None:
            r0, nr = r0 + rows[0], rows[1]
        return tuple(idx) + (pl.ds(r0, nr),)

    def with_core(idx, c):
        return (idx[0], c) + tuple(idx[1:])

    pieces = {}

    def piece(k, q, p):
        n = (k * 4 + q) * 3 + p
        a, b = ORDERS[p][:2]
        idx = place(p, around(a, k), around(b, q), slice(None))
        pieces[k, q, p] = idx, remote(w.at[with_core(idx, 1 - core)], acc.at[idx],
                                      in_send.at[n], in_recv.at[n], partner)

    def merge(k, q, p):
        idx, copy = pieces[k, q, p]
        copy.wait_recv()
        add(acc.at[idx], w.at[with_core(idx, core)], 4)

    share = SKETCH // 8
    mine = pl.ds((x * 2 + core) * share, share)

    def sum_start(s):
        first[s, x * 2 + core] = gram[s, mine, :]
        out = []
        for dx, dc in near:
            n = dx * 2 + dc
            to = around(2, dx) * 2 + ((1 - core) if dc else core)
            out.append(remote(gram.at[s, pl.ds(to * share, share)], first.at[s, x * 2 + core],
                              sum_send.at[s, n], sum_recv.at[s, n], near_device(dx, dc)))
        return out

    def landed(copies):
        for copy in copies:
            copy.wait_recv()

    def sum_along(s, a, value):
        cur[s, a] = value
        slots[s, a, me[a]] = value
        out = []
        for k in (1, 2, 3):
            n = 7 + a * 3 + k
            out.append(remote(cur.at[s, a], slots.at[s, a, me[a]], sum_send.at[s, n], sum_recv.at[s, n],
                              device(moved(a, k), core)))
        return out

    def sum_first(s, copies):
        landed(copies)
        v = [first[s, n] for n in range(8)]
        return ((v[0] + v[1]) + (v[2] + v[3])) + ((v[4] + v[5]) + (v[6] + v[7]))

    def sum_next(s, a, copies):
        landed(copies)
        return (slots[s, a, 0] + slots[s, a, 1]) + (slots[s, a, 2] + slots[s, a, 3])

    def sum_spread(s, value):
        cur[s, 2] = value
        total[s, mine, :] = value
        out = []
        for dx, dc in near:
            n = 13 + dx * 2 + dc
            out.append(remote(cur.at[s, 2], total.at[s, mine], sum_send.at[s, n], sum_recv.at[s, n],
                              near_device(dx, dc)))
        return out

    ring = {}

    def half(h):
        return pl.ds(2 * h, 2)

    def view(phase, p, q, coord, h):
        a, b, c = ORDERS[p]
        if phase == 0:
            return acc.at[place(p, coord, around(b, q), half(h))]
        if phase == 1:
            return acc.at[place(p, me[a], coord, half(h))]
        return acc.at[place(p, me[a], me[b], coord, tail(p, h))]

    def tail(p, h):
        return (0, 48) if h == 0 else (48, PARTS[p][1] - 48)

    def box(phase, p, q, m, h):
        nr = PARTS[p][1]
        if phase == 0:
            return box1.at[p, q, m, :, pl.ds(0, nr)]
        if phase == 1:
            return box2.at[p, m, :, pl.ds(0, nr)]
        return box3.at[p, m, pl.ds(0, tail(p, h)[1])]

    def send(phase, p, q, m):
        axis = ORDERS[p][phase]
        sign = 1 if m % 2 == 0 else -1
        h = TURN[m]
        n = (p * 4 + q) * 6 + m if phase == 0 else 72 + (phase - 1) * 18 + p * 6 + m
        ring[phase, p, q, m] = remote(
            view(phase, p, q, around(axis, 2 if m < 2 else sign), h), box(phase, p, q, m, h),
            ring_send.at[n], ring_recv.at[n], device(moved(axis, sign), core))

    def relay(phase, p, q, m):
        axis = ORDERS[p][phase]
        sign = 1 if m == 0 else -1
        ring[phase, p, q, m].wait_recv()
        add(view(phase, p, q, around(axis, sign), m), box(phase, p, q, m, m), 0 if phase == 2 else 2)
        send(phase, p, q, 4 + m)

    def land(phase, p, q, m):
        ring[phase, p, q, m].wait_recv()
        add(view(phase, p, q, me[ORDERS[p][phase]], TURN[m]), box(phase, p, q, m, TURN[m]),
            0 if phase == 2 else 2)

    def open_round(q):
        for p in range(3):
            merge(2, q, p)
            send(0, p, q, 0)
            send(0, p, q, 1)
        for p in range(3):
            merge(1, q, p)
            send(0, p, q, 2)
            merge(3, q, p)
            send(0, p, q, 3)

    def relay_round(q):
        for p in range(3):
            relay(0, p, q, 0)
            relay(0, p, q, 1)

    def close_round(q):
        for p in range(3):
            merge(0, q, p)
        for m in (2, 3, 4, 5):
            for p in range(3):
                land(0, p, q, m)
        for p in range(3):
            if q == 2:
                send(1, p, 0, 0)
                send(1, p, 0, 1)
            elif q == 1:
                send(1, p, 0, 2)
            elif q == 3:
                send(1, p, 0, 3)
        if q in (1, 3):
            for p in range(3):
                relay(1, p, 0, 0 if q == 1 else 1)

    for k in ROUNDS:
        for p in range(3):
            piece(k, 2, p)

    def gram_body(i, g):
        v = split[pl.ds(i * 8, 8)].reshape(8 * TILE, 2 * SKETCH)
        return g + lax.dot_general(v, v, (((0,), (0,)), ((), ())), preferred_element_type=F32)
    g = lax.fori_loop(0, CB_DEV // 8, gram_body, jnp.zeros((2 * SKETCH, 2 * SKETCH), F32))
    gram[0] = (g[:SKETCH, :SKETCH] + g[SKETCH:, SKETCH:]) + (g[:SKETCH, SKETCH:] + g[SKETCH:, :SKETCH])
    copies = sum_start(0)
    for q in ROUNDS[1:]:
        for k in ROUNDS:
            for p in range(3):
                piece(k, q, p)

    open_round(2)
    copies = sum_along(0, 1, sum_first(0, copies))
    open_round(1)
    relay_round(2)
    copies = sum_along(0, 0, sum_next(0, 1, copies))
    open_round(3)
    relay_round(1)
    close_round(2)
    copies = sum_spread(0, sum_next(0, 0, copies))
    open_round(0)
    relay_round(3)
    close_round(1)
    landed(copies)
    factor_start(total.at[0], work)
    factor_steps(work, inv1, 0, 5)
    relay_round(0)
    factor_steps(work, inv1, 5, 10)
    close_round(3)
    factor_steps(work, inv1, 10, 16)
    close_round(0)
    for m in (2, 3, 4, 5):
        for p in range(3):
            land(1, p, 0, m)
    for m in range(4):
        for p in range(3):
            send(2, p, 0, m)
    lh, ll = cut_two(inv1[...] * math.sqrt(CB_DEV * TILE * 128))
    weights = jnp.concatenate(
        [jnp.concatenate([lh, lh], axis=1), jnp.concatenate([ll, jnp.zeros_like(ll)], axis=1)], axis=0)
    for p in range(3):
        relay(2, p, 0, 0)
        relay(2, p, 0, 1)
    for m in (2, 3, 4, 5):
        for p in range(3):
            land(2, p, 0, m)

    zv = lax.dot_general(acc[z, y, x], inv1[...], (((1,), (1,)), ((), ())),
                         precision=HIGH, preferred_element_type=F32)
    zed[...] = zv
    gram[1] = lax.dot_general(zv, zv, (((0,), (0,)), ((), ())), precision=HIGH, preferred_element_type=F32)

    out_copies = []

    def cells(n):
        def body(i, carry):
            v = split[pl.ds(i * 4, 4)].reshape(4 * TILE, 2 * SKETCH)
            o = lax.dot_general(v, weights, (((1,), (1,)), ((), ())), preferred_element_type=F32)
            cell[pl.ds(pl.multiple_of(i * 4 * TILE, 4 * TILE), 4 * TILE), :] = (
                o[:, :SKETCH] + o[:, SKETCH:]).astype(BF16)
            return carry
        lax.fori_loop(n * 4, n * 4 + 4, body, 0)
        rows = pl.ds(n * 16 * TILE, 16 * TILE)
        copy = pltpu.make_async_copy(cell.at[rows], cell_out.at[rows], out_sem.at[n])
        copy.start()
        out_copies.append(copy)

    copies = sum_start(1)
    cells(0)
    copies = sum_along(1, 1, sum_first(1, copies))
    cells(1)
    copies = sum_along(1, 0, sum_next(1, 1, copies))
    cells(2)
    copies = sum_spread(1, sum_next(1, 0, copies))
    cells(3)
    landed(copies)
    factor_start(total.at[1], work)
    factor_steps(work, inv2, 0, 16)
    gene_out[...] = math.sqrt(GENES) * lax.dot_general(
        zed[...], inv2[...], (((1,), (1,)), ((), ())), precision=HIGH, preferred_element_type=F32)
    for copy in sends:
        copy.wait_send()
    for copy in out_copies:
        copy.wait()


def exchange(split, w):
    vmem = pl.BlockSpec(memory_space=pltpu.VMEM)
    sq = (SKETCH, SKETCH)
    part = (SKETCH // 8, SKETCH)
    return pl.pallas_call(
        exchange_kernel,
        name="exchange",
        out_shape=(
            jax.ShapeDtypeStruct((CB_DEV * TILE, SKETCH), BF16),
            jax.ShapeDtypeStruct((2 * TILE, SKETCH), F32),
        ),
        in_specs=[vmem, vmem],
        out_specs=(pl.BlockSpec(memory_space=pl.ANY), vmem),
        scratch_shapes=[
            pltpu.VMEM((4, 4, 4, 2 * TILE, SKETCH), F32),
            pltpu.VMEM((3, 4, 6, 2, 88, SKETCH), F32),
            pltpu.VMEM((3, 6, 2, 88, SKETCH), F32),
            pltpu.VMEM((3, 6, 48, SKETCH), F32),
            pltpu.VMEM((CB_DEV * TILE, SKETCH), BF16),
            pltpu.VMEM((2,) + sq, F32),
            pltpu.VMEM((2,) + sq, F32),
            pltpu.VMEM((SKETCH, 2 * SKETCH), F32),
            pltpu.VMEM(sq, F32),
            pltpu.VMEM(sq, F32),
            pltpu.VMEM((2 * TILE, SKETCH), F32),
            pltpu.VMEM((2, 3) + part, F32),
            pltpu.VMEM((2, 8) + part, F32),
            pltpu.VMEM((2, 2, 4) + part, F32),
            pltpu.SemaphoreType.DMA((48,)),
            pltpu.SemaphoreType.DMA((48,)),
            pltpu.SemaphoreType.DMA((108,)),
            pltpu.SemaphoreType.DMA((108,)),
            pltpu.SemaphoreType.DMA((2, 21)),
            pltpu.SemaphoreType.DMA((2, 21)),
            pltpu.SemaphoreType.DMA((4,)),
        ],
        compiler_params=pltpu.CompilerParams(
            collective_id=0, has_side_effects=True, vmem_limit_bytes=26 << 20),
    )(pltpu.with_memory_space_constraint(split, pltpu.VMEM), pltpu.with_memory_space_constraint(w, pltpu.VMEM))


def on_device(tiles, tile_rows, tile_cols, tile_counts, block_order, sketch):
    split, w = local_pass(tiles, tile_rows, tile_cols, tile_counts, block_order, sketch)
    return exchange(split, w)


def solution(mesh):
    placed = (
        P(("gx", "gy"), None, None),
        P(("gx", "gy")),
        P(("gx", "gy")),
        P(("gx", "gy")),
        P(),
        P(),
    )
    return jax.shard_map(
        on_device,
        mesh=mesh,
        in_specs=placed,
        out_specs=(P(("gx", "gy"), None), P(("gx", "gy"), None)),
        check_vma=False,
    )
```

time: 145 us -> 100 us (0.69)
  Pallas kernels: 125 us -> 96.7 us
  local copies, waits for them, and re-layouts: 18.3 us -> 1.98 us
    pallas_call x1, Pallas kernels: 113 us -> 84.3 us  [exchange(): pl.pallas_call(exchange_kernel, name='exchange', out_shape=(jax.ShapeDtyp...]
    unnamed x14 -> x2, local copies, waits for them, and re-layouts: 18.3 us -> 1.98 us
where the time goes in v2:
time: 100 us
  Pallas kernels  96.7 us (97%)
  local copies, waits for them, and re-layouts  1.98 us (2%)
  between operations  1.29 us (1%)
    pallas_call x1, Pallas kernels, exchange(): pl.pallas_call(exchange_kernel, name='exchange', out_shape=(jax.ShapeDtyp...  84.3 us
    pallas_call x1, Pallas kernels, local_pass(): pl.pallas_call(local_kernel, name='local_pass', out_shape=(pltpu.VMEM((CB...  12.4 us

profile of v2, /device:TPU:1, one launch (start us, length us, event | category | flops | bytes accessed | tf_op | source)
XLA Modules:
  0.0 100.0 jit_solution(11915940165537599106)
XLA Ops:
  1.3 12.4 %local_pass.1 = (bf16[64,128,256]{2,1,0:T(8,128)(2,1)S(1)}, f32[4,2,4,4,256,128]{5,4,3,2,1,0:T(8,128)S(1)}) custom-call(s32[1]{0:T(128)S(6)} %copy.10.counts, s32[192]{0:T(256)} %rows_hbm.1, s32[192]{0:T(256)} %cols_hbm.1, s32[256]{0:T(256)} %order_hbm.1, bf16[192,128,128]{2,1,0:T(8,128)(2,1)} %tiles_hbm.1, bf16[32768,128]{1,0:T(8,128)(2,1)} %sketch_hbm.1), custom_call_target="tpu_custom_call" | custom-call | tf_op jit(solution)/shard_map/local_pass/pallas_call | solution.py:126
  13.6 84.3 %exchange.1 = (bf16[8192,128]{1,0:T(8,128)(2,1)S(1)}, f32[256,128]{1,0:T(8,128)S(1)}) custom-call(bf16[64,128,256]{2,1,0:T(8,128)(2,1)S(1)} %get-tuple-element.4.split, f32[4,2,4,4,256,128]{5,4,3,2,1,0:T(8,128)S(1)} %get-tuple-element.5.w), custom_call_target="tpu_custom_call" | custom-call | tf_op jit(solution)/shard_map/exchange/pallas_call | solution.py:534
  98.0 1.3 %copy.11 = bf16[8192,128]{1,0:T(8,128)(2,1)} copy(bf16[8192,128]{1,0:T(8,128)(2,1)S(1)} %get-tuple-element.8) | data formatting | bytes 4194304
  99.3 0.7 copy.12

commit v3 on v2

--- a/solution.py
+++ b/solution.py
@@ -13,8 +13,8 @@
 CB_DEV = 64
 BLOCKS = 256
 SLOTS = 192
-GROUP = 8
-CHUNK = 16
+GROUP = 32
+CHUNK = 32
 F32 = jnp.float32
 BF16 = jnp.bfloat16
 
@@ -200,7 +200,7 @@
         ql = [(left[t] * inv[t])[:1] for t in range(WINDOW)]
         qr = [(right[t] * inv[t])[:1] for t in range(WINDOW)]
         ww = {k: v[:1] for k, v in w.items()}
-        for i in range(SKETCH // rows):
+        for i in range(first * 8 // rows, SKETCH // rows):
             here = pl.ds(i * rows, rows)
             a = work[here, :SKETCH]
             b = work[here, SKETCH:]
@@ -233,10 +233,10 @@
     lax.fori_loop(first, last, body, 0)
 
 
-def exchange_kernel(split, w, cell_out, gene_out,
-                    acc, box1, box2, box3, cell, gram, total, work, inv1, inv2, zed,
+def exchange_kernel(split, w, cell, zed, total2,
+                    acc, box1, box2, box3, gram, total, work, inv1,
                     cur, first, slots,
-                    in_send, in_recv, ring_send, ring_recv, sum_send, sum_recv, out_sem):
+                    in_send, in_recv, ring_send, ring_recv, sum_send, sum_recv):
     gx = lax.axis_index("gx")
     gy = lax.axis_index("gy")
     z, core = gx // 2, gx % 2
@@ -493,8 +493,6 @@
     zed[...] = zv
     gram[1] = lax.dot_general(zv, zv, (((0,), (0,)), ((), ())), precision=HIGH, preferred_element_type=F32)
 
-    out_copies = []
-
     def cells(n):
         def body(i, carry):
             v = split[pl.ds(i * 4, 4)].reshape(4 * TILE, 2 * SKETCH)
@@ -503,10 +501,6 @@
                 o[:, :SKETCH] + o[:, SKETCH:]).astype(BF16)
             return carry
         lax.fori_loop(n * 4, n * 4 + 4, body, 0)
-        rows = pl.ds(n * 16 * TILE, 16 * TILE)
-        copy = pltpu.make_async_copy(cell.at[rows], cell_out.at[rows], out_sem.at[n])
-        copy.start()
-        out_copies.append(copy)
 
     copies = sum_start(1)
     cells(0)
@@ -517,14 +511,20 @@
     copies = sum_spread(1, sum_next(1, 0, copies))
     cells(3)
     landed(copies)
-    factor_start(total.at[1], work)
-    factor_steps(work, inv2, 0, 16)
+    total2[...] = total[1]
+    for copy in sends:
+        copy.wait_send()
+
+
+def finish_kernel(cell, zed, gram, cell_out, gene_out, work, inv2, out_sem):
+    copy = pltpu.make_async_copy(cell, cell_out, out_sem.at[0])
+    copy.start()
+    factor_start(gram, work)
+    for n in range(4):
+        factor_steps(work, inv2, n * 4, n * 4 + 4)
     gene_out[...] = math.sqrt(GENES) * lax.dot_general(
         zed[...], inv2[...], (((1,), (1,)), ((), ())), precision=HIGH, preferred_element_type=F32)
-    for copy in sends:
-        copy.wait_send()
-    for copy in out_copies:
-        copy.wait()
+    copy.wait()
 
 
 def exchange(split, w):
@@ -535,23 +535,21 @@
         exchange_kernel,
         name="exchange",
         out_shape=(
-            jax.ShapeDtypeStruct((CB_DEV * TILE, SKETCH), BF16),
-            jax.ShapeDtypeStruct((2 * TILE, SKETCH), F32),
+            pltpu.VMEM((CB_DEV * TILE, SKETCH), BF16),
+            pltpu.VMEM((2 * TILE, SKETCH), F32),
+            pltpu.VMEM(sq, F32),
         ),
         in_specs=[vmem, vmem],
-        out_specs=(pl.BlockSpec(memory_space=pl.ANY), vmem),
+        out_specs=(vmem, vmem, vmem),
         scratch_shapes=[
             pltpu.VMEM((4, 4, 4, 2 * TILE, SKETCH), F32),
             pltpu.VMEM((3, 4, 6, 2, 88, SKETCH), F32),
             pltpu.VMEM((3, 6, 2, 88, SKETCH), F32),
             pltpu.VMEM((3, 6, 48, SKETCH), F32),
-            pltpu.VMEM((CB_DEV * TILE, SKETCH), BF16),
             pltpu.VMEM((2,) + sq, F32),
             pltpu.VMEM((2,) + sq, F32),
             pltpu.VMEM((SKETCH, 2 * SKETCH), F32),
             pltpu.VMEM(sq, F32),
-            pltpu.VMEM(sq, F32),
-            pltpu.VMEM((2 * TILE, SKETCH), F32),
             pltpu.VMEM((2, 3) + part, F32),
             pltpu.VMEM((2, 8) + part, F32),
             pltpu.VMEM((2, 2, 4) + part, F32),
@@ -561,16 +559,36 @@
             pltpu.SemaphoreType.DMA((108,)),
             pltpu.SemaphoreType.DMA((2, 21)),
             pltpu.SemaphoreType.DMA((2, 21)),
-            pltpu.SemaphoreType.DMA((4,)),
         ],
         compiler_params=pltpu.CompilerParams(
             collective_id=0, has_side_effects=True, vmem_limit_bytes=26 << 20),
     )(pltpu.with_memory_space_constraint(split, pltpu.VMEM), pltpu.with_memory_space_constraint(w, pltpu.VMEM))
 
 
+def finish(cell, zed, gram):
+    vmem = pl.BlockSpec(memory_space=pltpu.VMEM)
+    held = [pltpu.with_memory_space_constraint(v, pltpu.VMEM) for v in (cell, zed, gram)]
+    return pl.pallas_call(
+        finish_kernel,
+        name="finish",
+        out_shape=(
+            jax.ShapeDtypeStruct((CB_DEV * TILE, SKETCH), BF16),
+            jax.ShapeDtypeStruct((2 * TILE, SKETCH), F32),
+        ),
+        in_specs=[vmem, vmem, vmem],
+        out_specs=(pl.BlockSpec(memory_space=pl.ANY), vmem),
+        scratch_shapes=[
+            pltpu.VMEM((SKETCH, 2 * SKETCH), F32),
+            pltpu.VMEM((SKETCH, SKETCH), F32),
+            pltpu.SemaphoreType.DMA((1,)),
+        ],
+        compiler_params=pltpu.CompilerParams(vmem_limit_bytes=26 << 20),
+    )(*held)
+
+
 def on_device(tiles, tile_rows, tile_cols, tile_counts, block_order, sketch):
     split, w = local_pass(tiles, tile_rows, tile_cols, tile_counts, block_order, sketch)
-    return exchange(split, w)
+    return finish(*exchange(split, w))
 
 
 def solution(mesh):

time: 100 us -> 91.2 us (0.912)
  Pallas kernels: 96.7 us -> 89.8 us
  local copies, waits for them, and re-layouts: 1.98 us -> 0 us
    pallas_call x1 -> x2, Pallas kernels: 84.3 us -> 80.3 us  [the longest x1 72.9 us: exchange(): pl.pallas_call(exchange_kernel, name='exchange', out_shape=(pltpu.VMEM((C...]
    pallas_call x1, Pallas kernels: 12.4 us -> 9.48 us  [local_pass(): pl.pallas_call(local_kernel, name='local_pass', out_shape=(pltpu.VMEM((CB...]
    unnamed x2 -> x0, local copies, waits for them, and re-layouts: 1.98 us -> none
where the time goes in v3:
time: 91.2 us; the launch traced here: 91.1 us
  Pallas kernels  89.8 us (98%)
  between operations  1.29 us (1%)
    pallas_call x1, Pallas kernels, exchange(): pl.pallas_call(exchange_kernel, name='exchange', out_shape=(pltpu.VMEM((C...  72.9 us
    pallas_call x1, Pallas kernels, local_pass(): pl.pallas_call(local_kernel, name='local_pass', out_shape=(pltpu.VMEM((CB...  9.48 us
    pallas_call x1, Pallas kernels, finish(): pl.pallas_call(finish_kernel, name='finish', out_shape=(jax.ShapeDtypeStr...  7.37 us

profile of v3, /device:TPU:1, one launch (start us, length us, event | category | flops | bytes accessed | tf_op | source)
XLA Modules:
  0.0 91.1 jit_solution(17617441944171763949)
XLA Ops:
  1.3 9.5 %local_pass.1 = (bf16[64,128,256]{2,1,0:T(8,128)(2,1)S(1)}, f32[4,2,4,4,256,128]{5,4,3,2,1,0:T(8,128)S(1)}) custom-call(s32[1]{0:T(128)S(6)} %copy.8.counts, s32[192]{0:T(256)} %rows_hbm.1, s32[192]{0:T(256)} %cols_hbm.1, s32[256]{0:T(256)} %order_hbm.1, bf16[192,128,128]{2,1,0:T(8,128)(2,1)} %tiles_hbm.1, bf16[32768,128]{1,0:T(8,128)(2,1)} %sketch_hbm.1), custom_call_target="tpu_custom_call" | custom-call | tf_op jit(solution)/shard_map/local_pass/pallas_call | solution.py:126
  10.8 72.9 %exchange.1 = (bf16[8192,128]{1,0:T(8,128)(2,1)S(1)}, f32[256,128]{1,0:T(8,128)S(1)}, f32[128,128]{1,0:T(8,128)S(1)}) custom-call(bf16[64,128,256]{2,1,0:T(8,128)(2,1)S(1)} %get-tuple-element.7.split, f32[4,2,4,4,256,128]{5,4,3,2,1,0:T(8,128)S(1)} %get-tuple-element.8.w), custom_call_target="tpu_custom_call" | custom-call | tf_op jit(solution)/shard_map/exchange/pallas_call | solution.py:534
  83.7 7.4 %finish.1 = (bf16[8192,128]{1,0:T(8,128)(2,1)}, f32[256,128]{1,0:T(8,128)}) custom-call(bf16[8192,128]{1,0:T(8,128)(2,1)S(1)} %get-tuple-element.9.cell, f32[256,128]{1,0:T(8,128)S(1)} %get-tuple-element.10.zed, f32[128,128]{1,0:T(8,128)S(1)} %get-tuple-element.11.gram), custom_call_target="tpu_custom_call" | custom-call | tf_op jit(solution)/shard_map/finish/pallas_call | solution.py:571

commit v4 on v3

--- a/solution.py
+++ b/solution.py
@@ -13,8 +13,8 @@
 CB_DEV = 64
 BLOCKS = 256
 SLOTS = 192
-GROUP = 32
-CHUNK = 32
+GROUP = 64
+CHUNK = 64
 F32 = jnp.float32
 BF16 = jnp.bfloat16
 
@@ -153,7 +153,6 @@
 ROUNDS = (2, 1, 3, 0)
 TURN = (0, 1, 1, 0, 0, 1)
 MESH = pl.DeviceIdType.MESH
-HIGH = lax.Precision.HIGHEST
 
 
 def cut_two(v):
@@ -162,6 +161,26 @@
 
 
 WINDOW = 4
+
+
+def split_weights(inverse):
+    hi, lo = cut_two(inverse)
+    return jnp.concatenate(
+        [jnp.concatenate([hi, hi], axis=1), jnp.concatenate([lo, jnp.zeros_like(lo)], axis=1)], axis=0)
+
+
+def split_dot(terms, weights):
+    o = lax.dot_general(terms, weights, (((1,), (1,)), ((), ())), preferred_element_type=F32)
+    return o[:, :SKETCH] + o[:, SKETCH:]
+
+
+def split_gram(terms, g):
+    g = g + lax.dot_general(terms, terms, (((0,), (0,)), ((), ())), preferred_element_type=F32)
+    return g
+
+
+def fold(g):
+    return (g[:SKETCH, :SKETCH] + g[SKETCH:, SKETCH:]) + (g[:SKETCH, SKETCH:] + g[SKETCH:, :SKETCH])
 
 
 def factor_start(gram, work):
@@ -267,6 +286,7 @@
         pl.semaphore_signal(barrier, inc=1, device_id=peer, device_id_type=MESH)
     pl.semaphore_wait(barrier, len(peers))
 
+    scale = math.sqrt(CB_DEV * TILE * 128)
     sends = []
 
     def remote(src, dst, send, recv, peer):
@@ -278,21 +298,16 @@
         return copy
 
     def add(dst, src, lead):
-        if lead:
-            def body(i, carry):
-                dst[i] = dst[i] + src[i]
-                return carry
-            lax.fori_loop(0, lead, body, 0)
-        else:
-            dst[...] = dst[...] + src[...]
-
-    def place(p, ca, cb, cc, rows=None):
+        def body(i, carry):
+            dst[i] = dst[i] + src[i]
+            return carry
+        lax.fori_loop(0, lead, body, 0)
+
+    def place(p, ca, cb, cc):
         idx = [None] * 3
         for d, v in zip(ORDERS[p], (ca, cb, cc)):
             idx[d] = v
         r0, nr = PARTS[p]
-        if rows is not None:
-            r0, nr = r0 + rows[0], rows[1]
         return tuple(idx) + (pl.ds(r0, nr),)
 
     def with_core(idx, c):
@@ -367,20 +382,13 @@
         a, b, c = ORDERS[p]
         if phase == 0:
             return acc.at[place(p, coord, around(b, q), half(h))]
-        if phase == 1:
-            return acc.at[place(p, me[a], coord, half(h))]
-        return acc.at[place(p, me[a], me[b], coord, tail(p, h))]
-
-    def tail(p, h):
-        return (0, 48) if h == 0 else (48, PARTS[p][1] - 48)
+        return acc.at[place(p, me[a], coord, half(h))]
 
     def box(phase, p, q, m, h):
         nr = PARTS[p][1]
         if phase == 0:
             return box1.at[p, q, m, :, pl.ds(0, nr)]
-        if phase == 1:
-            return box2.at[p, m, :, pl.ds(0, nr)]
-        return box3.at[p, m, pl.ds(0, tail(p, h)[1])]
+        return box2.at[p, m, :, pl.ds(0, nr)]
 
     def send(phase, p, q, m):
         axis = ORDERS[p][phase]
@@ -395,24 +403,29 @@
         axis = ORDERS[p][phase]
         sign = 1 if m == 0 else -1
         ring[phase, p, q, m].wait_recv()
-        add(view(phase, p, q, around(axis, sign), m), box(phase, p, q, m, m), 0 if phase == 2 else 2)
+        add(view(phase, p, q, around(axis, sign), m), box(phase, p, q, m, m), 2)
         send(phase, p, q, 4 + m)
 
     def land(phase, p, q, m):
         ring[phase, p, q, m].wait_recv()
-        add(view(phase, p, q, me[ORDERS[p][phase]], TURN[m]), box(phase, p, q, m, TURN[m]),
-            0 if phase == 2 else 2)
-
-    def open_round(q):
+        add(view(phase, p, q, me[ORDERS[p][phase]], TURN[m]), box(phase, p, q, m, TURN[m]), 2)
+
+    def open_far(q):
         for p in range(3):
             merge(2, q, p)
             send(0, p, q, 0)
             send(0, p, q, 1)
+
+    def open_near(q):
         for p in range(3):
             merge(1, q, p)
             send(0, p, q, 2)
             merge(3, q, p)
             send(0, p, q, 3)
+
+    def open_round(q):
+        open_far(q)
+        open_near(q)
 
     def relay_round(q):
         for p in range(3):
@@ -441,18 +454,20 @@
         for p in range(3):
             piece(k, 2, p)
 
+    open_far(2)
+
     def gram_body(i, g):
         v = split[pl.ds(i * 8, 8)].reshape(8 * TILE, 2 * SKETCH)
-        return g + lax.dot_general(v, v, (((0,), (0,)), ((), ())), preferred_element_type=F32)
+        return split_gram(v, g)
     g = lax.fori_loop(0, CB_DEV // 8, gram_body, jnp.zeros((2 * SKETCH, 2 * SKETCH), F32))
-    gram[0] = (g[:SKETCH, :SKETCH] + g[SKETCH:, SKETCH:]) + (g[:SKETCH, SKETCH:] + g[SKETCH:, :SKETCH])
+    gram[0] = fold(g)
     copies = sum_start(0)
     for q in ROUNDS[1:]:
         for k in ROUNDS:
             for p in range(3):
                 piece(k, q, p)
 
-    open_round(2)
+    open_near(2)
     copies = sum_along(0, 1, sum_first(0, copies))
     open_round(1)
     relay_round(2)
@@ -475,30 +490,32 @@
     for m in (2, 3, 4, 5):
         for p in range(3):
             land(1, p, 0, m)
-    for m in range(4):
-        for p in range(3):
-            send(2, p, 0, m)
-    lh, ll = cut_two(inv1[...] * math.sqrt(CB_DEV * TILE * 128))
-    weights = jnp.concatenate(
-        [jnp.concatenate([lh, lh], axis=1), jnp.concatenate([ll, jnp.zeros_like(ll)], axis=1)], axis=0)
+    last = {}
+    for k in (2, 1, 3):
+        for p in range(3):
+            a, b, c = ORDERS[p]
+            n = 90 + p * 3 + k - 1
+            last[p, k] = remote(acc.at[place(p, me[a], me[b], around(c, k))],
+                                box3.at[p, k - 1, pl.ds(0, PARTS[p][1])],
+                                ring_send.at[n], ring_recv.at[n], device(moved(c, k), core))
+    weights = split_weights(inv1[...] * scale)
     for p in range(3):
-        relay(2, p, 0, 0)
-        relay(2, p, 0, 1)
-    for m in (2, 3, 4, 5):
-        for p in range(3):
-            land(2, p, 0, m)
-
-    zv = lax.dot_general(acc[z, y, x], inv1[...], (((1,), (1,)), ((), ())),
-                         precision=HIGH, preferred_element_type=F32)
+        a, b, c = ORDERS[p]
+        nr = PARTS[p][1]
+        for k in (1, 3, 2):
+            last[p, k].wait_recv()
+        own = acc.at[place(p, me[a], me[b], me[c])]
+        own[...] = (own[...] + box3[p, 0, :nr]) + (box3[p, 1, :nr] + box3[p, 2, :nr])
+
+    zv = split_dot(jnp.concatenate(cut_two(acc[z, y, x]), axis=1), weights) * (1.0 / scale)
+    zv = jnp.concatenate(cut_two(zv), axis=1)
     zed[...] = zv
-    gram[1] = lax.dot_general(zv, zv, (((0,), (0,)), ((), ())), precision=HIGH, preferred_element_type=F32)
+    gram[1] = fold(split_gram(zv, jnp.zeros((2 * SKETCH, 2 * SKETCH), F32)))
 
     def cells(n):
         def body(i, carry):
             v = split[pl.ds(i * 4, 4)].reshape(4 * TILE, 2 * SKETCH)
-            o = lax.dot_general(v, weights, (((1,), (1,)), ((), ())), preferred_element_type=F32)
-            cell[pl.ds(pl.multiple_of(i * 4 * TILE, 4 * TILE), 4 * TILE), :] = (
-                o[:, :SKETCH] + o[:, SKETCH:]).astype(BF16)
+            cell[pl.ds(pl.multiple_of(i * 4 * TILE, 4 * TILE), 4 * TILE), :] = split_dot(v, weights).astype(BF16)
             return carry
         lax.fori_loop(n * 4, n * 4 + 4, body, 0)
 
@@ -522,8 +539,7 @@
     factor_start(gram, work)
     for n in range(4):
         factor_steps(work, inv2, n * 4, n * 4 + 4)
-    gene_out[...] = math.sqrt(GENES) * lax.dot_general(
-        zed[...], inv2[...], (((1,), (1,)), ((), ())), precision=HIGH, preferred_element_type=F32)
+    gene_out[...] = split_dot(zed[...], split_weights(inv2[...] * math.sqrt(GENES)))
     copy.wait()
 
 
@@ -536,7 +552,7 @@
         name="exchange",
         out_shape=(
             pltpu.VMEM((CB_DEV * TILE, SKETCH), BF16),
-            pltpu.VMEM((2 * TILE, SKETCH), F32),
+            pltpu.VMEM((2 * TILE, 2 * SKETCH), BF16),
             pltpu.VMEM(sq, F32),
         ),
         in_specs=[vmem, vmem],
@@ -545,7 +561,7 @@
             pltpu.VMEM((4, 4, 4, 2 * TILE, SKETCH), F32),
             pltpu.VMEM((3, 4, 6, 2, 88, SKETCH), F32),
             pltpu.VMEM((3, 6, 2, 88, SKETCH), F32),
-            pltpu.VMEM((3, 6, 48, SKETCH), F32),
+            pltpu.VMEM((3, 3, 88, SKETCH), F32),
             pltpu.VMEM((2,) + sq, F32),
             pltpu.VMEM((2,) + sq, F32),
             pltpu.VMEM((SKETCH, 2 * SKETCH), F32),
@@ -555,8 +571,8 @@
             pltpu.VMEM((2, 2, 4) + part, F32),
             pltpu.SemaphoreType.DMA((48,)),
             pltpu.SemaphoreType.DMA((48,)),
-            pltpu.SemaphoreType.DMA((108,)),
-            pltpu.SemaphoreType.DMA((108,)),
+            pltpu.SemaphoreType.DMA((99,)),
+            pltpu.SemaphoreType.DMA((99,)),
             pltpu.SemaphoreType.DMA((2, 21)),
             pltpu.SemaphoreType.DMA((2, 21)),
         ],

time: 91.2 us -> 87.4 us (0.958)
  Pallas kernels: 89.8 us -> 86 us
    pallas_call x1, Pallas kernels: 9.48 us -> 7.56 us  [local_pass(): pl.pallas_call(local_kernel, name='local_pass', out_shape=(pltpu.VMEM((CB...]
    pallas_call x1, Pallas kernels: 72.9 us -> 71.1 us  [exchange(): pl.pallas_call(exchange_kernel, name='exchange', out_shape=(pltpu.VMEM((C...]
where the time goes in v4:
time: 87.4 us; the launch traced here: 87.3 us
  Pallas kernels  86 us (98%)
  between operations  1.29 us (1%)
    pallas_call x1, Pallas kernels, exchange(): pl.pallas_call(exchange_kernel, name='exchange', out_shape=(pltpu.VMEM((C...  71.1 us
    pallas_call x1, Pallas kernels, local_pass(): pl.pallas_call(local_kernel, name='local_pass', out_shape=(pltpu.VMEM((CB...  7.56 us
    pallas_call x1, Pallas kernels, finish(): pl.pallas_call(finish_kernel, name='finish', out_shape=(jax.ShapeDtypeStr...  7.31 us

profile of v4, /device:TPU:1, one launch (start us, length us, event | category | flops | bytes accessed | tf_op | source)
XLA Modules:
  0.0 87.3 jit_solution(2049879428696299465)
XLA Ops:
  1.3 7.6 %local_pass.1 = (bf16[64,128,256]{2,1,0:T(8,128)(2,1)S(1)}, f32[4,2,4,4,256,128]{5,4,3,2,1,0:T(8,128)S(1)}) custom-call(s32[1]{0:T(128)S(6)} %copy.8.counts, s32[192]{0:T(256)} %rows_hbm.1, s32[192]{0:T(256)} %cols_hbm.1, s32[256]{0:T(256)} %order_hbm.1, bf16[192,128,128]{2,1,0:T(8,128)(2,1)} %tiles_hbm.1, bf16[32768,128]{1,0:T(8,128)(2,1)} %sketch_hbm.1), custom_call_target="tpu_custom_call" | custom-call | tf_op jit(solution)/shard_map/local_pass/pallas_call | solution.py:126
  8.8 71.1 %exchange.1 = (bf16[8192,128]{1,0:T(8,128)(2,1)S(1)}, bf16[256,256]{1,0:T(8,128)(2,1)S(1)}, f32[128,128]{1,0:T(8,128)S(1)}) custom-call(bf16[64,128,256]{2,1,0:T(8,128)(2,1)S(1)} %get-tuple-element.7.split, f32[4,2,4,4,256,128]{5,4,3,2,1,0:T(8,128)S(1)} %get-tuple-element.8.w), custom_call_target="tpu_custom_call" | custom-call | tf_op jit(solution)/shard_map/exchange/pallas_call | solution.py:550
  80.0 7.3 %finish.1 = (bf16[8192,128]{1,0:T(8,128)(2,1)}, f32[256,128]{1,0:T(8,128)}) custom-call(bf16[8192,128]{1,0:T(8,128)(2,1)S(1)} %get-tuple-element.9.cell, bf16[256,256]{1,0:T(8,128)(2,1)S(1)} %get-tuple-element.10.zed, f32[128,128]{1,0:T(8,128)S(1)} %get-tuple-element.11.gram), custom_call_target="tpu_custom_call" | custom-call | tf_op jit(solution)/shard_map/finish/pallas_call | solution.py:587

commit v5 on v4

--- a/solution.py
+++ b/solution.py
@@ -468,11 +468,11 @@
                 piece(k, q, p)
 
     open_near(2)
+    open_round(1)
     copies = sum_along(0, 1, sum_first(0, copies))
-    open_round(1)
     relay_round(2)
+    open_round(3)
     copies = sum_along(0, 0, sum_next(0, 1, copies))
-    open_round(3)
     relay_round(1)
     close_round(2)
     copies = sum_spread(0, sum_next(0, 0, copies))

time: 87.4 us -> 86.7 us (level)
    pallas_call x1, Pallas kernels: 71.1 us -> 68.4 us  [exchange(): pl.pallas_call(exchange_kernel, name='exchange', out_shape=(pltpu.VMEM((C...]
    pallas_call x1, Pallas kernels: 7.56 us -> 9.6 us  [local_pass(): pl.pallas_call(local_kernel, name='local_pass', out_shape=(pltpu.VMEM((CB...]
where the time goes in v5:
time: 86.7 us; the launch traced here: 86.6 us
  Pallas kernels  85.3 us (98%)
  between operations  1.29 us (1%)
    pallas_call x1, Pallas kernels, exchange(): pl.pallas_call(exchange_kernel, name='exchange', out_shape=(pltpu.VMEM((C...  68.4 us
    pallas_call x1, Pallas kernels, local_pass(): pl.pallas_call(local_kernel, name='local_pass', out_shape=(pltpu.VMEM((CB...  9.6 us
    pallas_call x1, Pallas kernels, finish(): pl.pallas_call(finish_kernel, name='finish', out_shape=(jax.ShapeDtypeStr...  7.31 us

profile of v5, /device:TPU:1, one launch (start us, length us, event | category | flops | bytes accessed | tf_op | source)
XLA Modules:
  0.0 86.6 jit_solution(7669586449926487261)
XLA Ops:
  1.3 9.6 %local_pass.1 = (bf16[64,128,256]{2,1,0:T(8,128)(2,1)S(1)}, f32[4,2,4,4,256,128]{5,4,3,2,1,0:T(8,128)S(1)}) custom-call(s32[1]{0:T(128)S(6)} %copy.8.counts, s32[192]{0:T(256)} %rows_hbm.1, s32[192]{0:T(256)} %cols_hbm.1, s32[256]{0:T(256)} %order_hbm.1, bf16[192,128,128]{2,1,0:T(8,128)(2,1)} %tiles_hbm.1, bf16[32768,128]{1,0:T(8,128)(2,1)} %sketch_hbm.1), custom_call_target="tpu_custom_call" | custom-call | tf_op jit(solution)/shard_map/local_pass/pallas_call | solution.py:126
  10.9 68.4 %exchange.1 = (bf16[8192,128]{1,0:T(8,128)(2,1)S(1)}, bf16[256,256]{1,0:T(8,128)(2,1)S(1)}, f32[128,128]{1,0:T(8,128)S(1)}) custom-call(bf16[64,128,256]{2,1,0:T(8,128)(2,1)S(1)} %get-tuple-element.7.split, f32[4,2,4,4,256,128]{5,4,3,2,1,0:T(8,128)S(1)} %get-tuple-element.8.w), custom_call_target="tpu_custom_call" | custom-call | tf_op jit(solution)/shard_map/exchange/pallas_call | solution.py:550
  79.3 7.3 %finish.1 = (bf16[8192,128]{1,0:T(8,128)(2,1)}, f32[256,128]{1,0:T(8,128)}) custom-call(bf16[8192,128]{1,0:T(8,128)(2,1)S(1)} %get-tuple-element.9.cell, bf16[256,256]{1,0:T(8,128)(2,1)S(1)} %get-tuple-element.10.zed, f32[128,128]{1,0:T(8,128)S(1)} %get-tuple-element.11.gram), custom_call_target="tpu_custom_call" | custom-call | tf_op jit(solution)/shard_map/finish/pallas_call | solution.py:587

commit v6 on v5

--- a/solution.py
+++ b/solution.py
@@ -457,9 +457,9 @@
     open_far(2)
 
     def gram_body(i, g):
-        v = split[pl.ds(i * 8, 8)].reshape(8 * TILE, 2 * SKETCH)
+        v = split[pl.ds(i * 32, 32)].reshape(32 * TILE, 2 * SKETCH)
         return split_gram(v, g)
-    g = lax.fori_loop(0, CB_DEV // 8, gram_body, jnp.zeros((2 * SKETCH, 2 * SKETCH), F32))
+    g = lax.fori_loop(0, CB_DEV // 32, gram_body, jnp.zeros((2 * SKETCH, 2 * SKETCH), F32))
     gram[0] = fold(g)
     copies = sum_start(0)
     for q in ROUNDS[1:]:

time: 86.7 us -> 85.4 us (0.985)
  Pallas kernels: 85.3 us -> 84 us
    pallas_call x1, Pallas kernels: 68.4 us -> 67.1 us  [exchange(): pl.pallas_call(exchange_kernel, name='exchange', out_shape=(pltpu.VMEM((C...]
where the time goes in v6:
time: 85.4 us; the launch traced here: 85.3 us
  Pallas kernels  84 us (98%)
  between operations  1.29 us (2%)
    pallas_call x1, Pallas kernels, exchange(): pl.pallas_call(exchange_kernel, name='exchange', out_shape=(pltpu.VMEM((C...  67.1 us
    pallas_call x1, Pallas kernels, local_pass(): pl.pallas_call(local_kernel, name='local_pass', out_shape=(pltpu.VMEM((CB...  9.6 us
    pallas_call x1, Pallas kernels, finish(): pl.pallas_call(finish_kernel, name='finish', out_shape=(jax.ShapeDtypeStr...  7.32 us

profile of v6, /device:TPU:1, one launch (start us, length us, event | category | flops | bytes accessed | tf_op | source)
XLA Modules:
  0.0 85.3 jit_solution(6391167490685189027)
XLA Ops:
  1.3 9.6 %local_pass.1 = (bf16[64,128,256]{2,1,0:T(8,128)(2,1)S(1)}, f32[4,2,4,4,256,128]{5,4,3,2,1,0:T(8,128)S(1)}) custom-call(s32[1]{0:T(128)S(6)} %copy.8.counts, s32[192]{0:T(256)} %rows_hbm.1, s32[192]{0:T(256)} %cols_hbm.1, s32[256]{0:T(256)} %order_hbm.1, bf16[192,128,128]{2,1,0:T(8,128)(2,1)} %tiles_hbm.1, bf16[32768,128]{1,0:T(8,128)(2,1)} %sketch_hbm.1), custom_call_target="tpu_custom_call" | custom-call | tf_op jit(solution)/shard_map/local_pass/pallas_call | solution.py:126
  10.9 67.1 %exchange.1 = (bf16[8192,128]{1,0:T(8,128)(2,1)S(1)}, bf16[256,256]{1,0:T(8,128)(2,1)S(1)}, f32[128,128]{1,0:T(8,128)S(1)}) custom-call(bf16[64,128,256]{2,1,0:T(8,128)(2,1)S(1)} %get-tuple-element.7.split, f32[4,2,4,4,256,128]{5,4,3,2,1,0:T(8,128)S(1)} %get-tuple-element.8.w), custom_call_target="tpu_custom_call" | custom-call | tf_op jit(solution)/shard_map/exchange/pallas_call | solution.py:550
  78.0 7.3 %finish.1 = (bf16[8192,128]{1,0:T(8,128)(2,1)}, f32[256,128]{1,0:T(8,128)}) custom-call(bf16[8192,128]{1,0:T(8,128)(2,1)S(1)} %get-tuple-element.9.cell, bf16[256,256]{1,0:T(8,128)(2,1)S(1)} %get-tuple-element.10.zed, f32[128,128]{1,0:T(8,128)S(1)} %get-tuple-element.11.gram), custom_call_target="tpu_custom_call" | custom-call | tf_op jit(solution)/shard_map/finish/pallas_call | solution.py:587
